TPU v7x, 32 devices: a whole 2x2x4 slice. The times are simulated.
32 devices in a mesh: groups: 2 (over y), shot: 4 (over x, core), slab: 4 (over z).
Axes of the slice: x: 2, y: 2, z: 4, core: 2. Of those that a mesh axis runs over, the one named last changes fastest.
Arguments:
- slowness: float32 [32, 192, 128], P(('groups', 'slab')), parts along dimension 0, may hold values from 0.8 to 1.25
- wave_prev: float32 [8, 16, 192, 128], P(('groups', 'shot'), 'slab'), parts along dimension 0, may hold values from -6 to 6
- wave_now: float32 [8, 16, 192, 128], P(('groups', 'shot'), 'slab'), parts along dimension 0, may hold values from -6 to 6
- memory: float32 [8, 3, 16, 192, 128], P(('groups', 'shot'), None, 'slab'), parts along dimension 0, may hold values from -6 to 6
- adjoint_now: float32 [8, 16, 192, 128], P(('groups', 'shot'), 'slab'), parts along dimension 0, may hold values from -6 to 6
- adjoint_prev: float32 [8, 16, 192, 128], P(('groups', 'shot'), 'slab'), parts along dimension 0, may hold values from -6 to 6
- wavelet: float32 [4], replicated, may hold values from -16 to 16
- src_cells: int32 [8, 64], P(('groups', 'shot')), parts along dimension 0, may hold values from 0 to 393215
- src_signs: int32 [8, 64], P(('groups', 'shot')), parts along dimension 0, may hold values from -1 to 1, as said below
- rec_cells: int32 [512], P('groups'), parts along dimension 0, may hold values from 0 to 393215
- observed: float32 [8, 4, 256], P(('groups', 'shot')), parts along dimension 0, may hold values from -6 to 6
Outputs:
- new_slowness: float32 [32, 192, 128], P(('groups', 'slab')), parts along dimension 0
- gradient: float32 [32, 192, 128], P(('groups', 'slab'), 'shot'), parts along dimension 0
There are 2 independent parts, one for each index of `groups`. A program takes and returns all parts, laid end to end along the dimension named above; an argument that names none is the same for every part. Nothing has to cross between parts.
Inputs may be any that keep to these rules, and one draw needn't show every extreme that they name: `src_signs`: each entry is -1 or +1.
All inputs are finite; a program needn't handle non-finite values.
Results may differ from a plain program's by a relative error of at most 0.0001.
Values sent between devices are 32-bit elements; how exact they have to be, the bound alone decides.
No kernel may reach another device: no remote copies, remote signals or barrier semaphores. Data moves between devices by JAX's collectives and lax.ppermute only.
A program may use at most 64 MiB of HBM per device.

v0:
```python
import jax
import jax.numpy as jnp
from jax import lax
from jax.sharding import PartitionSpec as P

STEPS = 4
center_coef = -2.5
near_coef = 4.0 / 3.0
far_coef = -1.0 / 12.0
courant = 0.14
relax_decay = (0.3, 0.7, 0.95)
relax_weight = (0.3, 0.2, 0.1)
update_rate = 0.05
tiny_eps = 1e-06


def padded_2(block, sides, width):
    for axis, dim in sides:
        count = lax.axis_size(axis)
        forward = [(i, i + 1) for i in range(count - 1)]
        backward = [(target, source) for source, target in forward]
        low = lax.ppermute(
            lax.slice_in_dim(block, block.shape[dim] - width, None, axis=dim), axis, forward
        )
        high = lax.ppermute(lax.slice_in_dim(block, 0, width, axis=dim), axis, backward)
        block = jnp.concatenate([low, block, high], axis=dim)
    return block


def laplace(padded):
    middle = padded[2:-2]
    flanks = jnp.pad(middle, ((0, 0), (2, 2), (2, 2)))
    depth_sum = near_coef * (padded[3:-1] + padded[1:-3]) + far_coef * (padded[4:] + padded[:-4])
    cross_sum = near_coef * (flanks[:, 3:-1, 2:-2] + flanks[:, 1:-3, 2:-2]) + far_coef * (
        flanks[:, 4:, 2:-2] + flanks[:, :-4, 2:-2]
    )
    along_sum = near_coef * (flanks[:, 2:-2, 3:-1] + flanks[:, 2:-2, 1:-3]) + far_coef * (
        flanks[:, 2:-2, 4:] + flanks[:, 2:-2, :-4]
    )
    return 3.0 * center_coef * middle + depth_sum + cross_sum + along_sum


def place_sources(cells, signs, start, count):
    local = cells - start
    inside = (local >= 0) & (local < count)
    slot = jnp.where(inside, local, count)
    return jnp.zeros((count,), jnp.float32).at[slot].add(signs.astype(jnp.float32), mode="drop")


def per_device(
    slowness,
    wave_prev,
    wave_now,
    memory,
    adjoint_now,
    adjoint_prev,
    wavelet,
    src_cells,
    src_signs,
    rec_cells,
    observed,
):
    depth, width, lanes = slowness.shape
    plane = width * lanes
    block = depth * plane
    offset = lax.axis_index("slab") * block
    decay = jnp.array(relax_decay, jnp.float32)[:, None, None, None]
    weight = jnp.array(relax_weight, jnp.float32)[:, None, None, None]
    rec_local = rec_cells - offset
    rec_inside = (rec_local >= 0) & (rec_local < block)
    rec_slot = jnp.where(rec_inside, rec_local, block)
    rec_safe = jnp.minimum(rec_slot, block - 1)
    scaled = courant / (slowness * slowness)
    older, current, relax = (wave_prev[0], wave_now[0], memory[0])
    saved = []
    misfits = []

    def record(field, level):
        picked = field.reshape(-1)[rec_safe]
        misfits.append(jnp.where(rec_inside, picked - observed[0, level], 0.0))

    src_field = place_sources(src_cells[0], src_signs[0], offset, block).reshape(
        depth, width, lanes
    )
    for level in range(STEPS):
        padded = padded_2(current, (("slab", 0),), 2)
        curved = laplace(padded)
        accel = curved + jnp.sum(relax, 0)
        newer = 2.0 * current - older + scaled * accel + wavelet[level] * src_field
        relax = decay * relax - weight * curved[None]
        older, current = (current, newer)
        saved.append(accel)
        record(current, level)
    back_prev, back_now = (adjoint_prev[0], adjoint_now[0])
    back_relax = jnp.zeros_like(relax)
    accum = jnp.zeros_like(slowness)
    for level in reversed(range(STEPS)):
        inject = (
            jnp.zeros((block,), jnp.float32)
            .at[rec_slot]
            .add(misfits[level], mode="drop")
            .reshape(depth, width, lanes)
        )
        united = back_now + inject
        pushed = scaled * united
        drive = pushed - jnp.sum(weight * back_relax, 0)
        padded = padded_2(drive, (("slab", 0),), 2)
        accum = accum + united * saved[level]
        back_prev, back_now = (-united, back_prev + 2.0 * united + laplace(padded))
        back_relax = decay * back_relax + pushed[None]
    local_grad = accum * (-2.0 * courant / (slowness * slowness * slowness))
    cells_all = lax.axis_size("slab") * block
    share = width // lax.axis_size("shot")
    first = lax.axis_index("shot") * share
    summed = lax.psum(local_grad, "shot")
    squares = lax.psum(jnp.sum(summed * summed), "slab")
    rms_value = jnp.sqrt(squares / cells_all + tiny_eps)
    normed = summed / rms_value
    new_slowness = slowness - update_rate * normed
    gradient = lax.dynamic_slice_in_dim(normed, first, share, 1)
    return (new_slowness, gradient)


def solution(mesh):
    in_specs = (
        P(("groups", "slab"), None, None),
        P(("groups", "shot"), "slab", None, None),
        P(("groups", "shot"), "slab", None, None),
        P(("groups", "shot"), None, "slab", None, None),
        P(("groups", "shot"), "slab", None, None),
        P(("groups", "shot"), "slab", None, None),
        P(),
        P(("groups", "shot"), None),
        P(("groups", "shot"), None),
        P("groups"),
        P(("groups", "shot"), None, None),
    )
    out_specs = (P(("groups", "slab"), None, None), P(("groups", "slab"), "shot", None))
    return jax.shard_map(
        per_device, mesh=mesh, in_specs=in_specs, out_specs=out_specs, check_vma=False
    )
```

profile of v0, /device:TPU:0, one launch (start us, length us, event | category | flops | bytes accessed | tf_op | source)
XLA Modules:
  0.0 167.0 jit_solution(11458838551574252018)
XLA Ops:
  9.6 5.6 %collective-permute-start.1 = (f32[2,192,128]{2,1,0:T(8,128)S(1)}, f32[2,192,128]{2,1,0:T(8,128)S(1)}, u32[]{:S(2)}, u32[]{:S(2)}) collective-permute-start(f32[2,192,128]{2,1,0:T(8,128)S(1)} %get-tuple-element.43), channel_id=1, source_target_pairs={{0,1},{1,2},{2,3},{4,5},{5,6},{6,7},{8,9},{9,10},{10,11},{12,13},{... | collective-permute-start | bytes 589832 | tf_op jit(solution)/shard_map/ppermute | solution.py:22
  20.4 2.6 %broadcast_multiply_fusion.1 = (f32[98304]{0:T(1024)S(1)}, f32[98304]{0:T(1024)S(1)}, f32[98304]{0:T(1024)S(1)}, f32[98304]{0:T(1024)S(1)}) fusion(f32[98304]{0:T(1024)S(1)} %scatter_custom_fusion, f32[]{:T(128)} %bitcast.13, f32[]{:T(128)} %bitcast.15, f32[]{:T(128)} %bitcast.11, f32[]{:T(128)} %bitcast.5), kind=kLoop, calls=%fused_computation.281 | loop fusion | flops 393216 | bytes 1966096 | tf_op jit(solution)/shard_map/mul | solution.py:89
  25.8 4.6 %collective-permute-start.3 = (f32[2,192,128]{2,1,0:T(8,128)S(1)}, f32[2,192,128]{2,1,0:T(8,128)S(1)}, u32[]{:S(2)}, u32[]{:S(2)}) collective-permute-start(f32[2,192,128]{2,1,0:T(8,128)S(1)} %get-tuple-element.41), channel_id=1, source_target_pairs={{0,1},{1,2},{2,3},{4,5},{5,6},{6,7},{8,9},{9,10},{10,11},{12,13},{... | collective-permute-start | bytes 589832 | tf_op jit(solution)/shard_map/ppermute | solution.py:22
  30.6 2.1 %collective-permute-done.2 = f32[2,192,128]{2,1,0:T(8,128)S(1)} collective-permute-done((f32[2,192,128]{2,1,0:T(8,128)S(1)}, f32[2,192,128]{2,1,0:T(8,128)S(1)}, u32[]{:S(2)}, u32[]{:S(2)}) %collective-permute-start.2) | collective-permute-done | bytes 196640 | tf_op jit(solution)/shard_map/ppermute | solution.py:25
  35.8 5.0 %collective-permute-start.5 = (f32[2,192,128]{2,1,0:T(8,128)S(1)}, f32[2,192,128]{2,1,0:T(8,128)S(1)}, u32[]{:S(2)}, u32[]{:S(2)}) collective-permute-start(f32[2,192,128]{2,1,0:T(8,128)S(1)} %get-tuple-element.35), channel_id=1, source_target_pairs={{0,1},{1,2},{2,3},{4,5},{5,6},{6,7},{8,9},{9,10},{10,11},{12,13},{... | collective-permute-start | bytes 589832 | tf_op jit(solution)/shard_map/ppermute | solution.py:22
  47.2 5.0 %collective-permute-start.7 = (f32[2,192,128]{2,1,0:T(8,128)}, f32[2,192,128]{2,1,0:T(8,128)S(1)}, u32[]{:S(2)}, u32[]{:S(2)}) collective-permute-start(f32[2,192,128]{2,1,0:T(8,128)} %get-tuple-element.33), channel_id=1, source_target_pairs={{0,1},{1,2},{2,3},{4,5},{5,6},{6,7},{8,9},{9,10},{10,11},{12,13},{... | collective-permute-start | bytes 589832 | tf_op jit(solution)/shard_map/ppermute | solution.py:22
  52.8 2.3 %gather_fusion.3 = f32[256]{0:T(256)} fusion(f32[98304]{0:T(1024)S(1)} %bitcast.58, s32[1024]{0:T(1024)S(1)} %pad_clamp_fusion), kind=kCustom, calls=%fused_computation.3 | custom fusion | bytes 3072 | tf_op jit(solution)/shard_map/gather | solution.py:79
  55.2 2.3 %gather_fusion.2 = f32[256]{0:T(256)} fusion(f32[98304]{0:T(1024)S(1)} %bitcast.57, s32[1024]{0:T(1024)S(1)} %pad_clamp_fusion), kind=kCustom, calls=%fused_computation.2 | custom fusion | bytes 3072 | tf_op jit(solution)/shard_map/gather | solution.py:79
  57.5 2.3 %gather_fusion.1 = f32[256]{0:T(256)} fusion(f32[98304]{0:T(1024)S(1)} %bitcast.59, s32[1024]{0:T(1024)S(1)} %pad_clamp_fusion), kind=kCustom, calls=%fused_computation.1 | custom fusion | bytes 3072 | tf_op jit(solution)/shard_map/gather | solution.py:79
  60.5 1.6 add_add_fusion
  62.2 1.7 %gather_fusion = f32[256]{0:T(256)S(1)} fusion(f32[98304]{0:T(1024)S(1)} %bitcast.61, s32[1024]{0:T(1024)S(1)} %pad_clamp_fusion), kind=kCustom, calls=%fused_computation | custom fusion | bytes 3072 | tf_op jit(solution)/shard_map/gather | solution.py:79
  65.2 2.2 %scatter_custom_fusion.1 = f32[98304]{0:T(1024)S(1)} fusion(s32[256]{0:T(256)} %compare_select_fusion.1, f32[256]{0:T(256)S(1)} %get-tuple-element.51, f32[]{:T(128)} %constant.19.clone.1), kind=kCustom, calls=%fused_computation.292 | custom fusion | flops 256 | bytes 393728 | tf_op jit(solution)/shard_map/scatter-add | solution.py:101
  69.6 4.6 %collective-permute-start.9 = (f32[2,192,128]{2,1,0:T(8,128)}, f32[2,192,128]{2,1,0:T(8,128)S(1)}, u32[]{:S(2)}, u32[]{:S(2)}) collective-permute-start(f32[2,192,128]{2,1,0:T(8,128)} %get-tuple-element.31), channel_id=1, source_target_pairs={{0,1},{1,2},{2,3},{4,5},{5,6},{6,7},{8,9},{9,10},{10,11},{12,13},{... | collective-permute-start | bytes 589832 | tf_op jit(solution)/shard_map/ppermute | solution.py:22
  74.1 2.2 %scatter_custom_fusion.2 = f32[98304]{0:T(1024)S(1)} fusion(s32[256]{0:T(256)} %compare_select_fusion.1, f32[256]{0:T(256)} %get-tuple-element.50, f32[]{:T(128)} %constant.19.clone.1), kind=kCustom, calls=%fused_computation.290 | custom fusion | flops 256 | bytes 393728 | tf_op jit(solution)/shard_map/scatter-add | solution.py:101
  82.4 4.9 %collective-permute-start.11 = (f32[2,192,128]{2,1,0:T(8,128)S(1)}, f32[2,192,128]{2,1,0:T(8,128)S(1)}, u32[]{:S(2)}, u32[]{:S(2)}) collective-permute-start(f32[2,192,128]{2,1,0:T(8,128)S(1)} %get-tuple-element.29), channel_id=1, source_target_pairs={{0,1},{1,2},{2,3},{4,5},{5,6},{6,7},{8,9},{9,10},{10,11},{12,13},{... | collective-permute-start | bytes 589832 | tf_op jit(solution)/shard_map/ppermute | solution.py:22
  87.3 2.8 %scatter_custom_fusion.3 = f32[98304]{0:T(1024)} fusion(s32[256]{0:T(256)} %compare_select_fusion.1, f32[256]{0:T(256)} %get-tuple-element.48, f32[]{:T(128)} %constant.19.clone.1), kind=kCustom, calls=%fused_computation.288 | custom fusion | flops 256 | bytes 393728 | tf_op jit(solution)/shard_map/scatter-add | solution.py:101
  91.2 1.8 %multiply_subtract_fusion.2 = (f32[4,192,128]{2,1,0:T(8,128)S(1)}, f32[4,192,128]{2,1,0:T(8,128)S(1)}) fusion(f32[4,192,128]{2,1,0:T(8,128)} %get-tuple-element.5, f32[4,192,128]{2,1,0:T(8,128)S(1)} %copy-done, f32[4,192,128]{2,1,0:T(8,128)} %bitcast.66, f32[4,192,128]{2,1,0:T(8,128)S(1)} %fusion.169, f32[2,192,128]{2,1,0:T(8,128)} %copy-done.10, ...), kind=kLoop, calls=%fused_computation.275 | loop fusion | flops 3145728 | bytes 3538944 | tf_op jit(solution)/shard_map/sub | solution.py:106
  95.1 5.7 %collective-permute-start.13 = (f32[2,192,128]{2,1,0:T(8,128)}, f32[2,192,128]{2,1,0:T(8,128)}, u32[]{:S(2)}, u32[]{:S(2)}) collective-permute-start(f32[2,192,128]{2,1,0:T(8,128)} %get-tuple-element.27), channel_id=1, source_target_pairs={{0,1},{1,2},{2,3},{4,5},{5,6},{6,7},{8,9},{9,10},{10,11},{12,13},{... | collective-permute-start | bytes 589832 | tf_op jit(solution)/shard_map/ppermute | solution.py:22
  100.8 2.2 %scatter_custom_fusion.4 = f32[98304]{0:T(1024)S(1)} fusion(s32[256]{0:T(256)} %compare_select_fusion.1, f32[256]{0:T(256)S(1)} %get-tuple-element.49, f32[]{:T(128)} %constant.19.clone.1), kind=kCustom, calls=%fused_computation.286 | custom fusion | flops 256 | bytes 393728 | tf_op jit(solution)/shard_map/scatter-add | solution.py:101
  103.6 2.6 %fusion.4 = f32[4,192,128]{2,1,0:T(8,128)} fusion(f32[4,192,128]{2,1,0:T(8,128)S(1)} %copy-done, f32[4,192,128]{2,1,0:T(8,128)} %get-tuple-element.24, f32[4,192,128]{2,1,0:T(8,128)S(1)} %bitcast.65, f32[2,192,128]{2,1,0:T(8,128)} %collective-permute-done.13, f32[4,192,128]{2,1,0:T(8,128)S(1)} %get-tuple-element.8, ...), kind=kLoop, calls=%fused_computation.104 | loop fusion | flops 3833856 | bytes 4718592 | tf_op jit(solution)/shard_map/mul | solution.py:111
  106.2 36.8 %all-reduce.9.cloned.1.call-done = f32[4,192,128]{2,1,0:T(8,128)} async-done(((f32[4,192,128]{2,1,0:T(8,128)}), f32[4,192,128]{2,1,0:T(8,128)}) %all-reduce.9.cloned.1.call-update) | async-done | bytes 393232 | tf_op jit(solution)/shard_map/psum | solution.py:115
  143.0 1.7 %multiply_reduce_fusion.2 = f32[]{:T(128)} fusion(f32[4,192,128]{2,1,0:T(8,128)} %all-reduce.9.cloned.1.call-done), kind=kLoop, calls=%fused_computation.274 | loop fusion | flops 196607 | bytes 393220 | tf_op jit(solution)/shard_map/reduce_sum | solution.py:116
  144.7 12.3 %psum.15 = f32[]{:T(128)} all-reduce(f32[]{:T(128)} %multiply_reduce_fusion.2), channel_id=1, replica_groups=mesh['groups'=2,'shot'=4,'slab'=4] {'slab'}, use_global_device_ids=true, to_apply=%region_14.15 | all-reduce | flops 1 | bytes 8 | tf_op jit(solution)/shard_map/psum | solution.py:116
  157.7 1.8 %multiply_subtract_fusion.1 = (f32[4,192,128]{2,1,0:T(8,128)}, f32[4,192,128]{2,1,0:T(8,128)S(1)}) fusion(f32[4,192,128]{2,1,0:T(8,128)S(1)} %copy-done, f32[4,192,128]{2,1,0:T(8,128)} %all-reduce.9.cloned.1.call-done, f32[]{:T(128)S(6)} %sqrt.3), kind=kLoop, calls=%fused_computation.273 | loop fusion | flops 294912 | bytes 1572868 | tf_op jit(solution)/shard_map/sub | solution.py:119
  (84 shorter events, 35.0 us)
Async XLA Ops:
  7.2 135.9 %all-reduce.9.cloned.1.call-start = ((), (), s32[]{:S(2)}) async-start(), calls=%async_computation | async-start | bytes 786432 | tf_op jit(solution)/shard_map/psum | solution.py:115
  8.3 14.8 %collective-permute-start = (f32[2,192,128]{2,1,0:T(8,128)S(1)}, f32[2,192,128]{2,1,0:T(8,128)S(1)}, u32[]{:S(2)}, u32[]{:S(2)}) collective-permute-start(f32[2,192,128]{2,1,0:T(8,128)S(1)} %get-tuple-element.42), channel_id=1, source_target_pairs={{1,0},{2,1},{3,2},{5,4},{6,5},{7,6},{9,8},{10,9},{11,10},{13,12},{... | collective-permute-start | bytes 589832 | tf_op jit(solution)/shard_map/ppermute | solution.py:25
  9.6 13.5 %collective-permute-start.1 = (f32[2,192,128]{2,1,0:T(8,128)S(1)}, f32[2,192,128]{2,1,0:T(8,128)S(1)}, u32[]{:S(2)}, u32[]{:S(2)}) collective-permute-start(f32[2,192,128]{2,1,0:T(8,128)S(1)} %get-tuple-element.43), channel_id=1, source_target_pairs={{0,1},{1,2},{2,3},{4,5},{5,6},{6,7},{8,9},{9,10},{10,11},{12,13},{... | collective-permute-start | bytes 589832 | tf_op jit(solution)/shard_map/ppermute | solution.py:22
  19.3 3.8 %copy-start = (f32[4,192,128]{2,1,0:T(8,128)S(1)}, f32[4,192,128]{2,1,0:T(8,128)}, u32[]{:S(2)}) copy-start(f32[4,192,128]{2,1,0:T(8,128)} %param.13) | copy-start | bytes 1179652
  19.4 3.8 %copy-start.2 = (f32[1,4,192,128]{3,2,1,0:T(8,128)S(1)}, f32[1,4,192,128]{3,2,1,0:T(8,128)}, u32[]{:S(2)}) copy-start(f32[1,4,192,128]{3,2,1,0:T(8,128)} %param.15) | copy-start | bytes 1179652
  23.1 7.2 %copy-start.1 = (f32[1,3,4,192,128]{4,3,2,1,0:T(8,128)S(1)}, f32[1,3,4,192,128]{4,3,2,1,0:T(8,128)}, u32[]{:S(2)}) copy-start(f32[1,3,4,192,128]{4,3,2,1,0:T(8,128)} %param.16) | copy-start | bytes 3538948
  23.1 7.2 %copy-start.12 = (f32[3]{0:T(128)S(1)}, f32[3]{0:T(128)}, u32[]{:S(2)}) copy-start(f32[3]{0:T(128)} %constant.18.clone) | copy-start | bytes 40
  23.2 7.2 %copy-start.13 = (f32[3]{0:T(128)S(1)}, f32[3]{0:T(128)}, u32[]{:S(2)}) copy-start(f32[3]{0:T(128)} %constant.50.clone) | copy-start | bytes 40
  24.5 8.3 %collective-permute-start.2 = (f32[2,192,128]{2,1,0:T(8,128)S(1)}, f32[2,192,128]{2,1,0:T(8,128)S(1)}, u32[]{:S(2)}, u32[]{:S(2)}) collective-permute-start(f32[2,192,128]{2,1,0:T(8,128)S(1)} %get-tuple-element.40), channel_id=1, source_target_pairs={{1,0},{2,1},{3,2},{5,4},{6,5},{7,6},{9,8},{10,9},{11,10},{13,12},{... | collective-permute-start | bytes 589832 | tf_op jit(solution)/shard_map/ppermute | solution.py:25
  25.8 8.1 %collective-permute-start.3 = (f32[2,192,128]{2,1,0:T(8,128)S(1)}, f32[2,192,128]{2,1,0:T(8,128)S(1)}, u32[]{:S(2)}, u32[]{:S(2)}) collective-permute-start(f32[2,192,128]{2,1,0:T(8,128)S(1)} %get-tuple-element.41), channel_id=1, source_target_pairs={{0,1},{1,2},{2,3},{4,5},{5,6},{6,7},{8,9},{9,10},{10,11},{12,13},{... | collective-permute-start | bytes 589832 | tf_op jit(solution)/shard_map/ppermute | solution.py:22
  33.9 6.9 %copy-start.16 = (f32[1,4,256]{2,1,0:T(4,128)S(1)}, f32[1,4,256]{2,1,0:T(4,128)}, u32[]{:S(2)}) copy-start(f32[1,4,256]{2,1,0:T(4,128)} %param.23) | copy-start | bytes 12292
  34.5 8.0 %collective-permute-start.4 = (f32[2,192,128]{2,1,0:T(8,128)S(1)}, f32[2,192,128]{2,1,0:T(8,128)S(1)}, u32[]{:S(2)}, u32[]{:S(2)}) collective-permute-start(f32[2,192,128]{2,1,0:T(8,128)S(1)} %get-tuple-element.34), channel_id=1, source_target_pairs={{1,0},{2,1},{3,2},{5,4},{6,5},{7,6},{9,8},{10,9},{11,10},{13,12},{... | collective-permute-start | bytes 589832 | tf_op jit(solution)/shard_map/ppermute | solution.py:25
  35.8 8.2 %collective-permute-start.5 = (f32[2,192,128]{2,1,0:T(8,128)S(1)}, f32[2,192,128]{2,1,0:T(8,128)S(1)}, u32[]{:S(2)}, u32[]{:S(2)}) collective-permute-start(f32[2,192,128]{2,1,0:T(8,128)S(1)} %get-tuple-element.35), channel_id=1, source_target_pairs={{0,1},{1,2},{2,3},{4,5},{5,6},{6,7},{8,9},{9,10},{10,11},{12,13},{... | collective-permute-start | bytes 589832 | tf_op jit(solution)/shard_map/ppermute | solution.py:22
  45.0 7.3 %copy-start.15 = (s32[256]{0:T(256)S(1)}, s32[256]{0:T(256)}, u32[]{:S(2)}) copy-start(s32[256]{0:T(256)} %param.22) | copy-start | bytes 3076
  45.9 13.8 %collective-permute-start.6 = (f32[2,192,128]{2,1,0:T(8,128)}, f32[2,192,128]{2,1,0:T(8,128)S(1)}, u32[]{:S(2)}, u32[]{:S(2)}) collective-permute-start(f32[2,192,128]{2,1,0:T(8,128)} %get-tuple-element.32), channel_id=1, source_target_pairs={{1,0},{2,1},{3,2},{5,4},{6,5},{7,6},{9,8},{10,9},{11,10},{13,12},{... | collective-permute-start | bytes 589832 | tf_op jit(solution)/shard_map/ppermute | solution.py:25
  47.2 12.5 %collective-permute-start.7 = (f32[2,192,128]{2,1,0:T(8,128)}, f32[2,192,128]{2,1,0:T(8,128)S(1)}, u32[]{:S(2)}, u32[]{:S(2)}) collective-permute-start(f32[2,192,128]{2,1,0:T(8,128)} %get-tuple-element.33), channel_id=1, source_target_pairs={{0,1},{1,2},{2,3},{4,5},{5,6},{6,7},{8,9},{9,10},{10,11},{12,13},{... | collective-permute-start | bytes 589832 | tf_op jit(solution)/shard_map/ppermute | solution.py:22
  62.2 5.2 %copy-start.4 = (f32[1,4,192,128]{3,2,1,0:T(8,128)S(1)}, f32[1,4,192,128]{3,2,1,0:T(8,128)}, u32[]{:S(2)}) copy-start(f32[1,4,192,128]{3,2,1,0:T(8,128)} %param.17) | copy-start | bytes 1179652
  67.4 10.9 %copy-start.3 = (f32[1,4,192,128]{3,2,1,0:T(8,128)S(1)}, f32[1,4,192,128]{3,2,1,0:T(8,128)}, u32[]{:S(2)}) copy-start(f32[1,4,192,128]{3,2,1,0:T(8,128)} %param.18) | copy-start | bytes 1179652
  68.3 8.1 %collective-permute-start.8 = (f32[2,192,128]{2,1,0:T(8,128)}, f32[2,192,128]{2,1,0:T(8,128)S(1)}, u32[]{:S(2)}, u32[]{:S(2)}) collective-permute-start(f32[2,192,128]{2,1,0:T(8,128)} %get-tuple-element.30), channel_id=1, source_target_pairs={{1,0},{2,1},{3,2},{5,4},{6,5},{7,6},{9,8},{10,9},{11,10},{13,12},{... | collective-permute-start | bytes 589832 | tf_op jit(solution)/shard_map/ppermute | solution.py:25
  69.6 8.0 %collective-permute-start.9 = (f32[2,192,128]{2,1,0:T(8,128)}, f32[2,192,128]{2,1,0:T(8,128)S(1)}, u32[]{:S(2)}, u32[]{:S(2)}) collective-permute-start(f32[2,192,128]{2,1,0:T(8,128)} %get-tuple-element.31), channel_id=1, source_target_pairs={{0,1},{1,2},{2,3},{4,5},{5,6},{6,7},{8,9},{9,10},{10,11},{12,13},{... | collective-permute-start | bytes 589832 | tf_op jit(solution)/shard_map/ppermute | solution.py:22
  81.1 9.1 %collective-permute-start.10 = (f32[2,192,128]{2,1,0:T(8,128)S(1)}, f32[2,192,128]{2,1,0:T(8,128)S(1)}, u32[]{:S(2)}, u32[]{:S(2)}) collective-permute-start(f32[2,192,128]{2,1,0:T(8,128)S(1)} %get-tuple-element.28), channel_id=1, source_target_pairs={{1,0},{2,1},{3,2},{5,4},{6,5},{7,6},{9,8},{10,9},{11,10},{13,12},{... | collective-permute-start | bytes 589832 | tf_op jit(solution)/shard_map/ppermute | solution.py:25
  82.4 8.1 %collective-permute-start.11 = (f32[2,192,128]{2,1,0:T(8,128)S(1)}, f32[2,192,128]{2,1,0:T(8,128)S(1)}, u32[]{:S(2)}, u32[]{:S(2)}) collective-permute-start(f32[2,192,128]{2,1,0:T(8,128)S(1)} %get-tuple-element.29), channel_id=1, source_target_pairs={{0,1},{1,2},{2,3},{4,5},{5,6},{6,7},{8,9},{9,10},{10,11},{12,13},{... | collective-permute-start | bytes 589832 | tf_op jit(solution)/shard_map/ppermute | solution.py:22
  93.8 9.2 %collective-permute-start.12 = (f32[2,192,128]{2,1,0:T(8,128)}, f32[2,192,128]{2,1,0:T(8,128)}, u32[]{:S(2)}, u32[]{:S(2)}) collective-permute-start(f32[2,192,128]{2,1,0:T(8,128)} %get-tuple-element.26), channel_id=1, source_target_pairs={{1,0},{2,1},{3,2},{5,4},{6,5},{7,6},{9,8},{10,9},{11,10},{13,12},{... | collective-permute-start | bytes 589832 | tf_op jit(solution)/shard_map/ppermute | solution.py:25
  95.1 8.5 %collective-permute-start.13 = (f32[2,192,128]{2,1,0:T(8,128)}, f32[2,192,128]{2,1,0:T(8,128)}, u32[]{:S(2)}, u32[]{:S(2)}) collective-permute-start(f32[2,192,128]{2,1,0:T(8,128)} %get-tuple-element.27), channel_id=1, source_target_pairs={{0,1},{1,2},{2,3},{4,5},{5,6},{6,7},{8,9},{9,10},{10,11},{12,13},{... | collective-permute-start | bytes 589832 | tf_op jit(solution)/shard_map/ppermute | solution.py:22
  (8 other events, 12.2 us)
Sparse Core Ops, SparseCore 0:
  106.3 36.6 all-reduce.8
where the time goes:
time: 168 us; the launch traced here: 167 us
  waiting for transfers between devices  44.9 us (27%)
  starting transfers between devices  44.4 us (26%)
  other arithmetic  33.3 us (20%)
  local copies, waits for them, and re-layouts  17 us (10%)
  between operations  15.2 us (9%)
  blocking collectives  12.3 us (7%)
    psum x1, waiting for transfers between devices, per_device(): summed = lax.psum(local_grad, 'shot')  36.8 us
    ppermute x7, starting transfers between devices, padded_2(): lax.ppermute(lax.slice_in_dim(block, block.shape[dim] - width, None, axis...  35.4 us
    psum x1, blocking collectives, per_device(): squares = lax.psum(jnp.sum(summed * summed), 'slab')  12.3 us
    scatter-add x4, other arithmetic, per_device(): inject = jnp.zeros((block,), jnp.float32).at[rec_slot].add(misfits[level]...  9.37 us
    ppermute x7, starting transfers between devices, padded_2(): lax.ppermute(lax.slice_in_dim(block, 0, width, axis=dim), axis, backward)  9.01 us
    gather x4, local copies, waits for them, and re-layouts, record(): picked = field.reshape(-1)[rec_safe]  8.65 us
    ppermute x7, waiting for transfers between devices, padded_2(): lax.ppermute(lax.slice_in_dim(block, block.shape[dim] - width, None, axis...  4.85 us
    add x4, other arithmetic, per_device(): newer = 2.0 * current - older + scaled * accel + wavelet[level] * src_field  3.63 us
  transfers between devices with their start and end apart: 15, of which 8 were waited for; matrix products, arithmetic and copies ran while one was open for 14% of the time, Pallas kernels for 0%

commit v1 on v0

--- a/solution.py
+++ b/solution.py
@@ -112,7 +112,7 @@
     cells_all = lax.axis_size("slab") * block
     share = width // lax.axis_size("shot")
     first = lax.axis_index("shot") * share
-    summed = lax.psum(local_grad, "shot")
+    summed = jnp.sum(lax.all_gather(local_grad, "shot"), axis=0)
     squares = lax.psum(jnp.sum(summed * summed), "slab")
     rms_value = jnp.sqrt(squares / cells_all + tiny_eps)
     normed = summed / rms_value

time: 168 us -> 154 us (0.917)
  waiting for transfers between devices: 44.9 us -> 31.7 us
    psum x1 -> x0, waiting for transfers between devices: 36.8 us -> none  [per_device(): summed = lax.psum(local_grad, 'shot')]
    all_gather x0 -> x1, waiting for transfers between devices: none -> 23.7 us  [per_device(): summed = jnp.sum(lax.all_gather(local_grad, 'shot'), axis=0)]
  transfers between devices with their start and end apart: 15 -> 15, of which waited for: 8 -> 8; matrix products, arithmetic and copies ran while one was open for 14% -> 15% of each run, Pallas kernels for 0% -> 0%
where the time goes in v1:
time: 154 us; the launch traced here: 153 us
  starting transfers between devices  44.4 us (29%)
  other arithmetic  32.8 us (21%)
  waiting for transfers between devices  31.7 us (21%)
  local copies, waits for them, and re-layouts  17 us (11%)
  between operations  15.2 us (10%)
  blocking collectives  12.3 us (8%)
    ppermute x7, starting transfers between devices, padded_2(): lax.ppermute(lax.slice_in_dim(block, block.shape[dim] - width, None, axis...  35.4 us
    all_gather x1, waiting for transfers between devices, per_device(): summed = jnp.sum(lax.all_gather(local_grad, 'shot'), axis=0)  23.7 us
    psum x1, blocking collectives, per_device(): squares = lax.psum(jnp.sum(summed * summed), 'slab')  12.3 us
    scatter-add x4, other arithmetic, per_device(): inject = jnp.zeros((block,), jnp.float32).at[rec_slot].add(misfits[level]...  9.37 us
    ppermute x7, starting transfers between devices, padded_2(): lax.ppermute(lax.slice_in_dim(block, 0, width, axis=dim), axis, backward)  9.01 us
    gather x4, local copies, waits for them, and re-layouts, record(): picked = field.reshape(-1)[rec_safe]  8.65 us
    ppermute x7, waiting for transfers between devices, padded_2(): lax.ppermute(lax.slice_in_dim(block, block.shape[dim] - width, None, axis...  4.85 us
    add x4, other arithmetic, per_device(): newer = 2.0 * current - older + scaled * accel + wavelet[level] * src_field  3.63 us
  transfers between devices with their start and end apart: 15, of which 8 were waited for; matrix products, arithmetic and copies ran while one was open for 15% of the time, Pallas kernels for 0%

profile of v1, /device:TPU:0, one launch (start us, length us, event | category | flops | bytes accessed | tf_op | source)
XLA Modules:
  0.0 153.4 jit_solution(5797508484560830545)
XLA Ops:
  9.6 5.6 %collective-permute-start.1 = (f32[2,192,128]{2,1,0:T(8,128)S(1)}, f32[2,192,128]{2,1,0:T(8,128)S(1)}, u32[]{:S(2)}, u32[]{:S(2)}) collective-permute-start(f32[2,192,128]{2,1,0:T(8,128)S(1)} %get-tuple-element.43), channel_id=1, source_target_pairs={{0,1},{1,2},{2,3},{4,5},{5,6},{6,7},{8,9},{9,10},{10,11},{12,13},{... | collective-permute-start | bytes 589832 | tf_op jit(solution)/shard_map/ppermute | solution.py:22
  20.4 2.6 %broadcast_multiply_fusion.1 = (f32[98304]{0:T(1024)S(1)}, f32[98304]{0:T(1024)S(1)}, f32[98304]{0:T(1024)S(1)}, f32[98304]{0:T(1024)S(1)}) fusion(f32[98304]{0:T(1024)S(1)} %scatter_custom_fusion, f32[]{:T(128)} %bitcast.13, f32[]{:T(128)} %bitcast.15, f32[]{:T(128)} %bitcast.11, f32[]{:T(128)} %bitcast.5), kind=kLoop, calls=%fused_computation.281 | loop fusion | flops 393216 | bytes 1966096 | tf_op jit(solution)/shard_map/mul | solution.py:89
  25.8 4.6 %collective-permute-start.3 = (f32[2,192,128]{2,1,0:T(8,128)S(1)}, f32[2,192,128]{2,1,0:T(8,128)S(1)}, u32[]{:S(2)}, u32[]{:S(2)}) collective-permute-start(f32[2,192,128]{2,1,0:T(8,128)S(1)} %get-tuple-element.41), channel_id=1, source_target_pairs={{0,1},{1,2},{2,3},{4,5},{5,6},{6,7},{8,9},{9,10},{10,11},{12,13},{... | collective-permute-start | bytes 589832 | tf_op jit(solution)/shard_map/ppermute | solution.py:22
  30.6 2.1 %collective-permute-done.2 = f32[2,192,128]{2,1,0:T(8,128)S(1)} collective-permute-done((f32[2,192,128]{2,1,0:T(8,128)S(1)}, f32[2,192,128]{2,1,0:T(8,128)S(1)}, u32[]{:S(2)}, u32[]{:S(2)}) %collective-permute-start.2) | collective-permute-done | bytes 196640 | tf_op jit(solution)/shard_map/ppermute | solution.py:25
  35.8 5.0 %collective-permute-start.5 = (f32[2,192,128]{2,1,0:T(8,128)S(1)}, f32[2,192,128]{2,1,0:T(8,128)S(1)}, u32[]{:S(2)}, u32[]{:S(2)}) collective-permute-start(f32[2,192,128]{2,1,0:T(8,128)S(1)} %get-tuple-element.35), channel_id=1, source_target_pairs={{0,1},{1,2},{2,3},{4,5},{5,6},{6,7},{8,9},{9,10},{10,11},{12,13},{... | collective-permute-start | bytes 589832 | tf_op jit(solution)/shard_map/ppermute | solution.py:22
  47.2 5.0 %collective-permute-start.7 = (f32[2,192,128]{2,1,0:T(8,128)}, f32[2,192,128]{2,1,0:T(8,128)S(1)}, u32[]{:S(2)}, u32[]{:S(2)}) collective-permute-start(f32[2,192,128]{2,1,0:T(8,128)} %get-tuple-element.33), channel_id=1, source_target_pairs={{0,1},{1,2},{2,3},{4,5},{5,6},{6,7},{8,9},{9,10},{10,11},{12,13},{... | collective-permute-start | bytes 589832 | tf_op jit(solution)/shard_map/ppermute | solution.py:22
  52.8 2.3 %gather_fusion.3 = f32[256]{0:T(256)} fusion(f32[98304]{0:T(1024)S(1)} %bitcast.59, s32[1024]{0:T(1024)S(1)} %pad_clamp_fusion), kind=kCustom, calls=%fused_computation.3 | custom fusion | bytes 3072 | tf_op jit(solution)/shard_map/gather | solution.py:79
  55.2 2.3 %gather_fusion.2 = f32[256]{0:T(256)} fusion(f32[98304]{0:T(1024)S(1)} %bitcast.58, s32[1024]{0:T(1024)S(1)} %pad_clamp_fusion), kind=kCustom, calls=%fused_computation.2 | custom fusion | bytes 3072 | tf_op jit(solution)/shard_map/gather | solution.py:79
  57.5 2.3 %gather_fusion.1 = f32[256]{0:T(256)} fusion(f32[98304]{0:T(1024)S(1)} %bitcast.60, s32[1024]{0:T(1024)S(1)} %pad_clamp_fusion), kind=kCustom, calls=%fused_computation.1 | custom fusion | bytes 3072 | tf_op jit(solution)/shard_map/gather | solution.py:79
  60.5 1.6 %add_add_fusion = (f32[4,192,128]{2,1,0:T(8,128)S(1)}, f32[4,192,128]{2,1,0:T(8,128)S(1)}) fusion(f32[4,192,128]{2,1,0:T(8,128)S(1)} %bitcast.63, f32[4,192,128]{2,1,0:T(8,128)S(1)} %get-tuple-element.18, f32[4,192,128]{2,1,0:T(8,128)S(1)} %get-tuple-element.16, f32[4,192,128]{2,1,0:T(8,128)S(1)} %copy-done, f32[4,192,128]{2,1,0:T(8,128)S(1)} %get-tuple-element.3, ...), kind=kLoop, calls=%fused_computation.276 | loop fusion | flops 3047424 | bytes 3145728 | tf_op jit(solution)/shard_map/add | solution.py:89
  62.2 1.7 %gather_fusion = f32[256]{0:T(256)S(1)} fusion(f32[98304]{0:T(1024)S(1)} %bitcast.62, s32[1024]{0:T(1024)S(1)} %pad_clamp_fusion), kind=kCustom, calls=%fused_computation | custom fusion | bytes 3072 | tf_op jit(solution)/shard_map/gather | solution.py:79
  65.2 2.2 %scatter_custom_fusion.1 = f32[98304]{0:T(1024)S(1)} fusion(s32[256]{0:T(256)} %compare_select_fusion.1, f32[256]{0:T(256)S(1)} %get-tuple-element.51, f32[]{:T(128)} %constant.19.clone.1), kind=kCustom, calls=%fused_computation.292 | custom fusion | flops 256 | bytes 393728 | tf_op jit(solution)/shard_map/scatter-add | solution.py:101
  69.6 4.6 %collective-permute-start.9 = (f32[2,192,128]{2,1,0:T(8,128)}, f32[2,192,128]{2,1,0:T(8,128)S(1)}, u32[]{:S(2)}, u32[]{:S(2)}) collective-permute-start(f32[2,192,128]{2,1,0:T(8,128)} %get-tuple-element.31), channel_id=1, source_target_pairs={{0,1},{1,2},{2,3},{4,5},{5,6},{6,7},{8,9},{9,10},{10,11},{12,13},{... | collective-permute-start | bytes 589832 | tf_op jit(solution)/shard_map/ppermute | solution.py:22
  74.1 2.2 %scatter_custom_fusion.2 = f32[98304]{0:T(1024)S(1)} fusion(s32[256]{0:T(256)} %compare_select_fusion.1, f32[256]{0:T(256)} %get-tuple-element.50, f32[]{:T(128)} %constant.19.clone.1), kind=kCustom, calls=%fused_computation.290 | custom fusion | flops 256 | bytes 393728 | tf_op jit(solution)/shard_map/scatter-add | solution.py:101
  78.3 1.6 %fusion.167 = (f32[4,192,128]{2,1,0:T(8,128)S(1)}, f32[4,192,128]{2,1,0:T(8,128)S(1)}) fusion(f32[4,192,128]{2,1,0:T(8,128)S(1)} %copy-done, f32[4,192,128]{2,1,0:T(8,128)S(1)} %bitcast.68, f32[4,192,128]{2,1,0:T(8,128)S(1)} %get-tuple-element.12, f32[2,192,128]{2,1,0:T(8,128)} %copy-done.11, f32[2,192,128]{2,1,0:T(8,128)} %copy-done.9, ...), kind=kLoop, calls=%fused_computation.310 | loop fusion | flops 2949120 | bytes 3145728 | tf_op jit(solution)/shard_map/mul | solution.py:105
  82.4 4.9 %collective-permute-start.11 = (f32[2,192,128]{2,1,0:T(8,128)S(1)}, f32[2,192,128]{2,1,0:T(8,128)S(1)}, u32[]{:S(2)}, u32[]{:S(2)}) collective-permute-start(f32[2,192,128]{2,1,0:T(8,128)S(1)} %get-tuple-element.29), channel_id=1, source_target_pairs={{0,1},{1,2},{2,3},{4,5},{5,6},{6,7},{8,9},{9,10},{10,11},{12,13},{... | collective-permute-start | bytes 589832 | tf_op jit(solution)/shard_map/ppermute | solution.py:22
  87.3 2.8 %scatter_custom_fusion.3 = f32[98304]{0:T(1024)} fusion(s32[256]{0:T(256)} %compare_select_fusion.1, f32[256]{0:T(256)} %get-tuple-element.48, f32[]{:T(128)} %constant.19.clone.1), kind=kCustom, calls=%fused_computation.288 | custom fusion | flops 256 | bytes 393728 | tf_op jit(solution)/shard_map/scatter-add | solution.py:101
  91.2 1.8 %multiply_subtract_fusion.2 = (f32[4,192,128]{2,1,0:T(8,128)S(1)}, f32[4,192,128]{2,1,0:T(8,128)S(1)}) fusion(f32[4,192,128]{2,1,0:T(8,128)} %get-tuple-element.5, f32[4,192,128]{2,1,0:T(8,128)S(1)} %copy-done, f32[4,192,128]{2,1,0:T(8,128)} %bitcast.67, f32[4,192,128]{2,1,0:T(8,128)S(1)} %fusion.169, f32[2,192,128]{2,1,0:T(8,128)} %copy-done.10, ...), kind=kLoop, calls=%fused_computation.275 | loop fusion | flops 3145728 | bytes 3538944 | tf_op jit(solution)/shard_map/sub | solution.py:106
  95.1 5.7 %collective-permute-start.13 = (f32[2,192,128]{2,1,0:T(8,128)}, f32[2,192,128]{2,1,0:T(8,128)}, u32[]{:S(2)}, u32[]{:S(2)}) collective-permute-start(f32[2,192,128]{2,1,0:T(8,128)} %get-tuple-element.27), channel_id=1, source_target_pairs={{0,1},{1,2},{2,3},{4,5},{5,6},{6,7},{8,9},{9,10},{10,11},{12,13},{... | collective-permute-start | bytes 589832 | tf_op jit(solution)/shard_map/ppermute | solution.py:22
  100.8 2.2 %scatter_custom_fusion.4 = f32[98304]{0:T(1024)S(1)} fusion(s32[256]{0:T(256)} %compare_select_fusion.1, f32[256]{0:T(256)S(1)} %get-tuple-element.49, f32[]{:T(128)} %constant.19.clone.1), kind=kCustom, calls=%fused_computation.286 | custom fusion | flops 256 | bytes 393728 | tf_op jit(solution)/shard_map/scatter-add | solution.py:101
  103.6 2.6 %fusion.4 = f32[4,192,128]{2,1,0:T(8,128)} fusion(f32[4,192,128]{2,1,0:T(8,128)S(1)} %copy-done, f32[4,192,128]{2,1,0:T(8,128)} %get-tuple-element.24, f32[4,192,128]{2,1,0:T(8,128)S(1)} %bitcast.66, f32[2,192,128]{2,1,0:T(8,128)} %collective-permute-done.13, f32[4,192,128]{2,1,0:T(8,128)S(1)} %get-tuple-element.8, ...), kind=kLoop, calls=%fused_computation.104 | loop fusion | flops 3833856 | bytes 4718592 | tf_op jit(solution)/shard_map/mul | solution.py:111
  106.2 23.7 %all-gather.3.cloned.1.call-done = f32[16,192,128]{2,1,0:T(8,128)} async-done(((f32[4,192,128]{2,1,0:T(8,128)}), f32[16,192,128]{2,1,0:T(8,128)}) %all-gather.3.cloned.1.call-update) | async-done | bytes 1572880 | tf_op jit(solution)/shard_map/all_gather | solution.py:115
  129.9 1.5 reduce_sum.91
  132.1 12.3 %psum.7 = f32[]{:T(128)} all-reduce(f32[]{:T(128)} %multiply_reduce_fusion.2), channel_id=1, replica_groups=mesh['groups'=2,'shot'=4,'slab'=4] {'slab'}, use_global_device_ids=true, to_apply=%region_14.15 | all-reduce | flops 1 | bytes 8 | tf_op jit(solution)/shard_map/psum | solution.py:116
  (85 shorter events, 34.9 us)
Async XLA Ops:
  7.2 122.7 %all-gather.3.cloned.1.call-start = ((), (), s32[]{:S(2)}) async-start(), calls=%async_computation | async-start | bytes 1966080 | tf_op jit(solution)/shard_map/all_gather | solution.py:115
  8.3 14.8 %collective-permute-start = (f32[2,192,128]{2,1,0:T(8,128)S(1)}, f32[2,192,128]{2,1,0:T(8,128)S(1)}, u32[]{:S(2)}, u32[]{:S(2)}) collective-permute-start(f32[2,192,128]{2,1,0:T(8,128)S(1)} %get-tuple-element.42), channel_id=1, source_target_pairs={{1,0},{2,1},{3,2},{5,4},{6,5},{7,6},{9,8},{10,9},{11,10},{13,12},{... | collective-permute-start | bytes 589832 | tf_op jit(solution)/shard_map/ppermute | solution.py:25
  9.6 13.5 %collective-permute-start.1 = (f32[2,192,128]{2,1,0:T(8,128)S(1)}, f32[2,192,128]{2,1,0:T(8,128)S(1)}, u32[]{:S(2)}, u32[]{:S(2)}) collective-permute-start(f32[2,192,128]{2,1,0:T(8,128)S(1)} %get-tuple-element.43), channel_id=1, source_target_pairs={{0,1},{1,2},{2,3},{4,5},{5,6},{6,7},{8,9},{9,10},{10,11},{12,13},{... | collective-permute-start | bytes 589832 | tf_op jit(solution)/shard_map/ppermute | solution.py:22
  19.3 3.8 %copy-start = (f32[4,192,128]{2,1,0:T(8,128)S(1)}, f32[4,192,128]{2,1,0:T(8,128)}, u32[]{:S(2)}) copy-start(f32[4,192,128]{2,1,0:T(8,128)} %param.13) | copy-start | bytes 1179652
  19.4 3.8 %copy-start.2 = (f32[1,4,192,128]{3,2,1,0:T(8,128)S(1)}, f32[1,4,192,128]{3,2,1,0:T(8,128)}, u32[]{:S(2)}) copy-start(f32[1,4,192,128]{3,2,1,0:T(8,128)} %param.15) | copy-start | bytes 1179652
  23.1 7.2 %copy-start.1 = (f32[1,3,4,192,128]{4,3,2,1,0:T(8,128)S(1)}, f32[1,3,4,192,128]{4,3,2,1,0:T(8,128)}, u32[]{:S(2)}) copy-start(f32[1,3,4,192,128]{4,3,2,1,0:T(8,128)} %param.16) | copy-start | bytes 3538948
  23.1 7.2 %copy-start.12 = (f32[3]{0:T(128)S(1)}, f32[3]{0:T(128)}, u32[]{:S(2)}) copy-start(f32[3]{0:T(128)} %constant.18.clone) | copy-start | bytes 40
  23.2 7.2 %copy-start.13 = (f32[3]{0:T(128)S(1)}, f32[3]{0:T(128)}, u32[]{:S(2)}) copy-start(f32[3]{0:T(128)} %constant.50.clone) | copy-start | bytes 40
  24.5 8.3 %collective-permute-start.2 = (f32[2,192,128]{2,1,0:T(8,128)S(1)}, f32[2,192,128]{2,1,0:T(8,128)S(1)}, u32[]{:S(2)}, u32[]{:S(2)}) collective-permute-start(f32[2,192,128]{2,1,0:T(8,128)S(1)} %get-tuple-element.40), channel_id=1, source_target_pairs={{1,0},{2,1},{3,2},{5,4},{6,5},{7,6},{9,8},{10,9},{11,10},{13,12},{... | collective-permute-start | bytes 589832 | tf_op jit(solution)/shard_map/ppermute | solution.py:25
  25.8 8.1 %collective-permute-start.3 = (f32[2,192,128]{2,1,0:T(8,128)S(1)}, f32[2,192,128]{2,1,0:T(8,128)S(1)}, u32[]{:S(2)}, u32[]{:S(2)}) collective-permute-start(f32[2,192,128]{2,1,0:T(8,128)S(1)} %get-tuple-element.41), channel_id=1, source_target_pairs={{0,1},{1,2},{2,3},{4,5},{5,6},{6,7},{8,9},{9,10},{10,11},{12,13},{... | collective-permute-start | bytes 589832 | tf_op jit(solution)/shard_map/ppermute | solution.py:22
  33.9 6.9 %copy-start.16 = (f32[1,4,256]{2,1,0:T(4,128)S(1)}, f32[1,4,256]{2,1,0:T(4,128)}, u32[]{:S(2)}) copy-start(f32[1,4,256]{2,1,0:T(4,128)} %param.23) | copy-start | bytes 12292
  34.5 8.0 %collective-permute-start.4 = (f32[2,192,128]{2,1,0:T(8,128)S(1)}, f32[2,192,128]{2,1,0:T(8,128)S(1)}, u32[]{:S(2)}, u32[]{:S(2)}) collective-permute-start(f32[2,192,128]{2,1,0:T(8,128)S(1)} %get-tuple-element.34), channel_id=1, source_target_pairs={{1,0},{2,1},{3,2},{5,4},{6,5},{7,6},{9,8},{10,9},{11,10},{13,12},{... | collective-permute-start | bytes 589832 | tf_op jit(solution)/shard_map/ppermute | solution.py:25
  35.8 8.2 %collective-permute-start.5 = (f32[2,192,128]{2,1,0:T(8,128)S(1)}, f32[2,192,128]{2,1,0:T(8,128)S(1)}, u32[]{:S(2)}, u32[]{:S(2)}) collective-permute-start(f32[2,192,128]{2,1,0:T(8,128)S(1)} %get-tuple-element.35), channel_id=1, source_target_pairs={{0,1},{1,2},{2,3},{4,5},{5,6},{6,7},{8,9},{9,10},{10,11},{12,13},{... | collective-permute-start | bytes 589832 | tf_op jit(solution)/shard_map/ppermute | solution.py:22
  45.0 7.3 %copy-start.15 = (s32[256]{0:T(256)S(1)}, s32[256]{0:T(256)}, u32[]{:S(2)}) copy-start(s32[256]{0:T(256)} %param.22) | copy-start | bytes 3076
  45.9 13.8 %collective-permute-start.6 = (f32[2,192,128]{2,1,0:T(8,128)}, f32[2,192,128]{2,1,0:T(8,128)S(1)}, u32[]{:S(2)}, u32[]{:S(2)}) collective-permute-start(f32[2,192,128]{2,1,0:T(8,128)} %get-tuple-element.32), channel_id=1, source_target_pairs={{1,0},{2,1},{3,2},{5,4},{6,5},{7,6},{9,8},{10,9},{11,10},{13,12},{... | collective-permute-start | bytes 589832 | tf_op jit(solution)/shard_map/ppermute | solution.py:25
  47.2 12.5 %collective-permute-start.7 = (f32[2,192,128]{2,1,0:T(8,128)}, f32[2,192,128]{2,1,0:T(8,128)S(1)}, u32[]{:S(2)}, u32[]{:S(2)}) collective-permute-start(f32[2,192,128]{2,1,0:T(8,128)} %get-tuple-element.33), channel_id=1, source_target_pairs={{0,1},{1,2},{2,3},{4,5},{5,6},{6,7},{8,9},{9,10},{10,11},{12,13},{... | collective-permute-start | bytes 589832 | tf_op jit(solution)/shard_map/ppermute | solution.py:22
  62.2 5.2 %copy-start.4 = (f32[1,4,192,128]{3,2,1,0:T(8,128)S(1)}, f32[1,4,192,128]{3,2,1,0:T(8,128)}, u32[]{:S(2)}) copy-start(f32[1,4,192,128]{3,2,1,0:T(8,128)} %param.17) | copy-start | bytes 1179652
  67.4 10.9 %copy-start.3 = (f32[1,4,192,128]{3,2,1,0:T(8,128)S(1)}, f32[1,4,192,128]{3,2,1,0:T(8,128)}, u32[]{:S(2)}) copy-start(f32[1,4,192,128]{3,2,1,0:T(8,128)} %param.18) | copy-start | bytes 1179652
  68.3 8.1 %collective-permute-start.8 = (f32[2,192,128]{2,1,0:T(8,128)}, f32[2,192,128]{2,1,0:T(8,128)S(1)}, u32[]{:S(2)}, u32[]{:S(2)}) collective-permute-start(f32[2,192,128]{2,1,0:T(8,128)} %get-tuple-element.30), channel_id=1, source_target_pairs={{1,0},{2,1},{3,2},{5,4},{6,5},{7,6},{9,8},{10,9},{11,10},{13,12},{... | collective-permute-start | bytes 589832 | tf_op jit(solution)/shard_map/ppermute | solution.py:25
  69.6 8.0 %collective-permute-start.9 = (f32[2,192,128]{2,1,0:T(8,128)}, f32[2,192,128]{2,1,0:T(8,128)S(1)}, u32[]{:S(2)}, u32[]{:S(2)}) collective-permute-start(f32[2,192,128]{2,1,0:T(8,128)} %get-tuple-element.31), channel_id=1, source_target_pairs={{0,1},{1,2},{2,3},{4,5},{5,6},{6,7},{8,9},{9,10},{10,11},{12,13},{... | collective-permute-start | bytes 589832 | tf_op jit(solution)/shard_map/ppermute | solution.py:22
  81.1 9.1 %collective-permute-start.10 = (f32[2,192,128]{2,1,0:T(8,128)S(1)}, f32[2,192,128]{2,1,0:T(8,128)S(1)}, u32[]{:S(2)}, u32[]{:S(2)}) collective-permute-start(f32[2,192,128]{2,1,0:T(8,128)S(1)} %get-tuple-element.28), channel_id=1, source_target_pairs={{1,0},{2,1},{3,2},{5,4},{6,5},{7,6},{9,8},{10,9},{11,10},{13,12},{... | collective-permute-start | bytes 589832 | tf_op jit(solution)/shard_map/ppermute | solution.py:25
  82.4 8.1 %collective-permute-start.11 = (f32[2,192,128]{2,1,0:T(8,128)S(1)}, f32[2,192,128]{2,1,0:T(8,128)S(1)}, u32[]{:S(2)}, u32[]{:S(2)}) collective-permute-start(f32[2,192,128]{2,1,0:T(8,128)S(1)} %get-tuple-element.29), channel_id=1, source_target_pairs={{0,1},{1,2},{2,3},{4,5},{5,6},{6,7},{8,9},{9,10},{10,11},{12,13},{... | collective-permute-start | bytes 589832 | tf_op jit(solution)/shard_map/ppermute | solution.py:22
  93.8 9.2 %collective-permute-start.12 = (f32[2,192,128]{2,1,0:T(8,128)}, f32[2,192,128]{2,1,0:T(8,128)}, u32[]{:S(2)}, u32[]{:S(2)}) collective-permute-start(f32[2,192,128]{2,1,0:T(8,128)} %get-tuple-element.26), channel_id=1, source_target_pairs={{1,0},{2,1},{3,2},{5,4},{6,5},{7,6},{9,8},{10,9},{11,10},{13,12},{... | collective-permute-start | bytes 589832 | tf_op jit(solution)/shard_map/ppermute | solution.py:25
  95.1 8.5 %collective-permute-start.13 = (f32[2,192,128]{2,1,0:T(8,128)}, f32[2,192,128]{2,1,0:T(8,128)}, u32[]{:S(2)}, u32[]{:S(2)}) collective-permute-start(f32[2,192,128]{2,1,0:T(8,128)} %get-tuple-element.27), channel_id=1, source_target_pairs={{0,1},{1,2},{2,3},{4,5},{5,6},{6,7},{8,9},{9,10},{10,11},{12,13},{... | collective-permute-start | bytes 589832 | tf_op jit(solution)/shard_map/ppermute | solution.py:22
  (8 other events, 12.2 us)
Sparse Core Ops, SparseCore 0:
  106.3 23.4 all-gather.2
